TPU v7x, 512 devices: a whole 4x4x16 slice. The times are simulated.
512 devices in a mesh: replica: 64 (over y, z), tensor: 8 (over x, core).
Axes of the slice: x: 4, y: 4, z: 16, core: 2. Of those that a mesh axis runs over, the one named last changes fastest.
Arguments:
- prefill_q: bfloat16 [24576, 8192], P('replica', 'tensor'), may hold values from -16 to 16
- decode_q: bfloat16 [128, 8192], P('replica', 'tensor'), may hold values from -16 to 16
- overflow_q: bfloat16 [1536, 8192], P('replica', 'tensor'), may hold values from -16 to 16
- key_pool: bfloat16 [417792, 1024], P('replica', 'tensor'), may hold values from -10 to 10
- value_pool: bfloat16 [417792, 1024], P('replica', 'tensor'), may hold values from -6 to 6
- prefill_pages: int32 [64, 19], P('replica'), may hold values from 0 to 50, as said below
- decode_pages: int32 [128, 4], P('replica'), may hold values from 0 to 50, as said below
- decode_len: int32 [128], P('replica'), may hold values from 1 to 512, as said below
- overflow_pages: int32 [1536], P('replica'), may hold values from 0 to 50, as said below
- overflow_len: int32 [1536], P('replica'), may hold values from 1 to 128, as said below
- overflow_dest: int32 [1536], P('replica'), may hold values from 0 to 63, as said below
Outputs:
- prefill_out: bfloat16 [24576, 8192], P(('replica', 'tensor'))
- decode_out: bfloat16 [128, 8192], P('replica', 'tensor')
- moved_out: bfloat16 [4096, 8192], P('replica', 'tensor')
Inputs may be any that keep to these rules, and one draw needn't show every extreme that they name: The page lists of one replica (prefill_pages, decode_pages and overflow_pages together) name distinct pages of that replica's pool. `decode_pages`: distinct pages of the own pool, as for prefill_pages. `overflow_pages`: distinct pages of the own pool, as for prefill_pages. `decode_len`: every replica has a decoding request of exactly 512 positions. `overflow_len`: every replica has an overflow request of exactly 128 positions. `overflow_dest`: the requests of one replica go to distinct replicas other than itself; one replica receives a request from every other replica.
All inputs are finite; a program needn't handle non-finite values.
Results may differ from a plain program's by a relative error of at most 0.0049.
Values may be sent and summed in bfloat16 or wider, within the bound.
A program may use at most 64 MiB of HBM per device.

v0:
```python
import math

import jax
import jax.numpy as jnp
from jax import lax
from jax.sharding import PartitionSpec as P

Q_HEADS = 64
KV_HEADS = 8
D_HEAD = 128
PAGE = 128


def score_block(queries, key_rows, value_rows, usable):
    scores = jnp.einsum(
        "bngqd,blgd->bgqnl", queries, key_rows, preferred_element_type=jnp.float32
    ) / math.sqrt(D_HEAD)
    scores = jnp.where(usable[:, None, None], scores, -1e30)
    maxima = jnp.max(scores, axis=-1, keepdims=True)
    expon = jnp.exp(scores - maxima)
    weights = (expon / jnp.sum(expon, axis=-1, keepdims=True)).astype(jnp.bfloat16)
    return jnp.einsum(
        "bgqnl,blgd->bngqd", weights, value_rows, preferred_element_type=jnp.float32
    ).astype(jnp.bfloat16)


def attend_rows(queries, key_rows, value_rows, usable):
    batch = queries.shape[0]
    heads_kv = key_rows.shape[-1] // D_HEAD
    per_group = Q_HEADS // KV_HEADS
    q_five = queries.reshape(batch, 1, heads_kv, per_group, D_HEAD)
    k_four = key_rows.reshape(batch, -1, heads_kv, D_HEAD)
    v_four = value_rows.reshape(batch, -1, heads_kv, D_HEAD)
    result = score_block(q_five, k_four, v_four, usable[:, None, :])
    return result.reshape(batch, -1)


def prefill_heads(prefill_q, key_pages, value_pages, page_list):
    tokens = prefill_q.shape[0]
    heads_kv = key_pages.shape[-1] // D_HEAD
    per_group = Q_HEADS // KV_HEADS
    key_span = page_list.shape[0] * key_pages.shape[1]
    key_rows = key_pages[page_list].reshape(1, key_span, heads_kv, D_HEAD)
    value_rows = value_pages[page_list].reshape(1, key_span, heads_kv, D_HEAD)
    earlier = key_span - tokens
    usable = (jnp.arange(key_span)[None, :] <= earlier + jnp.arange(tokens)[:, None])[None]
    q_blocks = prefill_q.reshape(tokens, heads_kv, per_group // 2, 2, D_HEAD).transpose(
        2, 0, 1, 3, 4
    )

    def head_pair(q_block):
        return score_block(q_block[None], key_rows, value_rows, usable)[0]

    results = lax.map(head_pair, q_blocks)
    return results.transpose(1, 2, 0, 3, 4).reshape(tokens, -1)


def per_device(
    prefill_q,
    decode_q,
    overflow_q,
    key_pool,
    value_pool,
    prefill_pages,
    decode_pages,
    decode_len,
    overflow_pages,
    overflow_len,
    overflow_dest,
):
    width_kv = key_pool.shape[1]
    page_rows = key_pool.shape[0] // PAGE
    key_pages = key_pool.reshape(page_rows, PAGE, width_kv)
    value_pages = value_pool.reshape(page_rows, PAGE, width_kv)
    local_heads = prefill_heads(prefill_q, key_pages, value_pages, prefill_pages[0])
    prefill_out = lax.all_to_all(local_heads, "tensor", split_axis=0, concat_axis=1, tiled=True)
    dec_count = decode_q.shape[0]
    dec_span = decode_pages.shape[1] * PAGE
    dec_keys = key_pages[decode_pages].reshape(dec_count, dec_span, width_kv)
    dec_values = value_pages[decode_pages].reshape(dec_count, dec_span, width_kv)
    dec_usable = jnp.arange(dec_span)[None, :] < decode_len[:, None]
    decode_out = attend_rows(decode_q, dec_keys, dec_values, dec_usable)
    replicas = lax.axis_size("replica")
    listing = overflow_dest[None, :] == jnp.arange(replicas, dtype=jnp.int32)[:, None]
    present = jnp.any(listing, axis=1)
    chosen = jnp.sum(
        jnp.where(listing, jnp.arange(overflow_dest.shape[0], dtype=jnp.int32)[None, :], 0), axis=1
    )
    send_pages = overflow_pages[chosen]
    send_keys = key_pages[send_pages]
    send_values = value_pages[send_pages]
    send_q = overflow_q[chosen]
    send_len = jnp.where(present, overflow_len[chosen], 0).astype(jnp.bfloat16)
    got_keys, got_values, got_q, got_len = (
        lax.all_to_all(send_keys, "replica", split_axis=0, concat_axis=0, tiled=True),
        lax.all_to_all(send_values, "replica", split_axis=0, concat_axis=0, tiled=True),
        lax.all_to_all(send_q, "replica", split_axis=0, concat_axis=0, tiled=True),
        lax.all_to_all(send_len, "replica", split_axis=0, concat_axis=0, tiled=True),
    )
    got_count = got_len.astype(jnp.int32)
    got_usable = jnp.arange(PAGE)[None, :] < got_count[:, None]
    landed = attend_rows(got_q, got_keys, got_values, got_usable)
    moved_out = jnp.where((got_count > 0)[:, None], landed, jnp.zeros_like(landed))
    return (prefill_out, decode_out, moved_out)


def solution(mesh):
    in_specs = (
        P("replica", "tensor"),
        P("replica", "tensor"),
        P("replica", "tensor"),
        P("replica", "tensor"),
        P("replica", "tensor"),
        P("replica", None),
        P("replica", None),
        P("replica"),
        P("replica"),
        P("replica"),
        P("replica"),
    )
    out_specs = (P(("replica", "tensor"), None), P("replica", "tensor"), P("replica", "tensor"))
    return jax.shard_map(
        per_device, mesh=mesh, in_specs=in_specs, out_specs=out_specs, check_vma=False
    )
```

profile of v0, /device:TPU:1, one launch (start us, length us, event | category | flops | bytes accessed | tf_op | source)
XLA Modules:
  0.0 324.4 jit_solution(9639734607087740746)
XLA Ops:
  3.0 1.4 gather_fusion.4
  5.1 19.3 %all-to-all-start.1 = ((bf16[64,1,1]{2,1,0:T(2,128)(2,1)}), bf16[64,1,1]{2,1,0:T(2,128)(2,1)S(1)}, u32[]{:S(2)}, u32[]{:S(2)}) async-start(bf16[64,1,1]{2,1,0:T(2,128)(2,1)} %copy.37), calls=%async_computation.1 | async-start | bytes 65536 | tf_op jit(solution)/shard_map/all_to_all | solution.py:98
  25.0 2.3 copy.33
  27.3 1.5 gather_fusion
  28.8 1.5 gather_fusion.1
  31.8 1.4 reduce.9
  33.1 1.6 reshape.354
  34.7 2.9 all-to-all-done.1
  37.7 11.6 %all-to-all-start.4 = ((bf16[64,2,512]{2,1,0:T(2,128)(2,1)}), bf16[64,2,512]{2,1,0:T(2,128)(2,1)S(1)}, u32[]{:S(2)}, u32[]{:S(2)}) async-start(bf16[64,2,512]{2,1,0:T(2,128)(2,1)} %reshape.354), calls=%async_computation.4 | async-start | bytes 262144 | tf_op jit(solution)/shard_map/all_to_all | solution.py:97
  49.3 32.1 %while.11 = (s32[]{:T(128)}, bf16[4,384,1,2,128]{4,1,3,2,0:T(8,128)(2,1)}, bf16[4,384,1,2,128]{1,4,3,0,2:T(8,128)(2,1)}, bf16[1,2432,1,128]{3,1,2,0:T(8,128)(2,1...) while((s32[]{:T(128)}, bf16[4,384,1,2,128]{4,1,3,2,0:T(8,128)(2,1)}, ...), condition=%wide.region_3.4_spmd.clone, body=%wide.region_0.3_spmd.clone.sunk | while | flops 972274176 | bytes 28426872 | solution.py:54
  50.6 3.3 %fusion.53 = (f32[2,384]{1,0:T(2,128)S(1)}, f32[1,1,2,384,2432]{4,3,2,1,0:T(8,128)S(1)}) fusion(bf16[1,2432,1,128]{3,1,2,0:T(8,128)(2,1)} %get-tuple-element.157, bf16[4,384,1,2,128]{1,4,3,0,2:T(8,128)(2,1)} %get-tuple-element.156, s32[]{:T(128)S(6)} %copy.58, pred[384,2432]{1,0:T(8,128)(4,1)S(1)} %iota_compare_fusion.5), kind=kOutput, calls=%fused_computation.70.clone.1 | convolution fusion | flops 483753216 | bytes 9227268 | tf_op jit(solution)/shard_map/while/body/eval_jaxpr/bngqd,blgd->bgqnl/dot_general | solution.py:15
  55.0 2.3 fusion.55
  58.6 3.3 %fusion.53 = (f32[2,384]{1,0:T(2,128)S(1)}, f32[1,1,2,384,2432]{4,3,2,1,0:T(8,128)S(1)}) fusion(bf16[1,2432,1,128]{3,1,2,0:T(8,128)(2,1)} %get-tuple-element.157, bf16[4,384,1,2,128]{1,4,3,0,2:T(8,128)(2,1)} %get-tuple-element.156, s32[]{:T(128)S(6)} %copy.58, pred[384,2432]{1,0:T(8,128)(4,1)S(1)} %iota_compare_fusion.5), kind=kOutput, calls=%fused_computation.70.clone.1 | convolution fusion | flops 483753216 | bytes 9227268 | tf_op jit(solution)/shard_map/while/body/eval_jaxpr/bngqd,blgd->bgqnl/dot_general | solution.py:15
  63.1 2.3 fusion.55
  66.6 3.3 %fusion.53 = (f32[2,384]{1,0:T(2,128)S(1)}, f32[1,1,2,384,2432]{4,3,2,1,0:T(8,128)S(1)}) fusion(bf16[1,2432,1,128]{3,1,2,0:T(8,128)(2,1)} %get-tuple-element.157, bf16[4,384,1,2,128]{1,4,3,0,2:T(8,128)(2,1)} %get-tuple-element.156, s32[]{:T(128)S(6)} %copy.58, pred[384,2432]{1,0:T(8,128)(4,1)S(1)} %iota_compare_fusion.5), kind=kOutput, calls=%fused_computation.70.clone.1 | convolution fusion | flops 483753216 | bytes 9227268 | tf_op jit(solution)/shard_map/while/body/eval_jaxpr/bngqd,blgd->bgqnl/dot_general | solution.py:15
  71.1 2.3 fusion.55
  74.7 3.3 %fusion.53 = (f32[2,384]{1,0:T(2,128)S(1)}, f32[1,1,2,384,2432]{4,3,2,1,0:T(8,128)S(1)}) fusion(bf16[1,2432,1,128]{3,1,2,0:T(8,128)(2,1)} %get-tuple-element.157, bf16[4,384,1,2,128]{1,4,3,0,2:T(8,128)(2,1)} %get-tuple-element.156, s32[]{:T(128)S(6)} %copy.58, pred[384,2432]{1,0:T(8,128)(4,1)S(1)} %iota_compare_fusion.5), kind=kOutput, calls=%fused_computation.70.clone.1 | convolution fusion | flops 483753216 | bytes 9227268 | tf_op jit(solution)/shard_map/while/body/eval_jaxpr/bngqd,blgd->bgqnl/dot_general | solution.py:15
  79.1 2.3 fusion.55
  81.4 2.8 copy.35
  84.2 3.1 all_to_all.30
  87.4 5.8 %all-to-all-start = ((bf16[8,48,1024]{2,1,0:T(8,128)(2,1)}), bf16[8,48,1024]{2,1,0:T(8,128)(2,1)}, u32[]{:S(2)}, u32[]{:S(2)}) async-start(bf16[8,48,1024]{2,1,0:T(8,128)(2,1)} %all_to_all.30), calls=%async_computation | async-start | bytes 1572864 | tf_op jit(solution)/shard_map/all_to_all | solution.py:76
  94.1 2.1 gather_fusion.7
  96.2 9.3 %all-to-all-done = bf16[8,48,1024]{2,1,0:T(8,128)(2,1)} async-done(((bf16[8,48,1024]{2,1,0:T(8,128)(2,1)}), bf16[8,48,1024]{2,1,0:T(8,128)(2,1)}, u32[]{:S(2)}, u32[]{:S(2)}) %all-to-all-start) | async-done | bytes 786464 | tf_op jit(solution)/shard_map/all_to_all | solution.py:76
  105.6 15.3 %all-to-all-start.3 = ((bf16[64,128,128]{2,1,0:T(8,128)(2,1)}), bf16[64,128,128]{2,1,0:T(8,128)(2,1)}, u32[]{:S(2)}, u32[]{:S(2)}) async-start(bf16[64,128,128]{2,1,0:T(8,128)(2,1)} %gather_fusion.7), calls=%async_computation.3 | async-start | bytes 4194304 | tf_op jit(solution)/shard_map/all_to_all | solution.py:95
  120.9 2.1 gather_fusion.6
  123.0 89.3 %all-to-all-done.3 = bf16[64,128,128]{2,1,0:T(8,128)(2,1)} async-done(((bf16[64,128,128]{2,1,0:T(8,128)(2,1)}), bf16[64,128,128]{2,1,0:T(8,128)(2,1)}, u32[]{:S(2)}, u32[]{:S(2)}) %all-to-all-start.3) | async-done | bytes 2097184 | tf_op jit(solution)/shard_map/all_to_all | solution.py:95
  212.3 14.2 %all-to-all-start.2 = ((bf16[64,128,128]{2,1,0:T(8,128)(2,1)}), bf16[64,128,128]{2,1,0:T(8,128)(2,1)}, u32[]{:S(2)}, u32[]{:S(2)}) async-start(bf16[64,128,128]{2,1,0:T(8,128)(2,1)} %gather_fusion.6), calls=%async_computation.2 | async-start | bytes 4194304 | tf_op jit(solution)/shard_map/all_to_all | solution.py:96
  227.8 1.3 gather_fusion.3
  234.6 2.1 copy.40
  236.6 2.9 fusion.40
  239.7 81.6 %all-to-all-done.2 = bf16[64,128,128]{2,1,0:T(8,128)(2,1)} async-done(((bf16[64,128,128]{2,1,0:T(8,128)(2,1)}), bf16[64,128,128]{2,1,0:T(8,128)(2,1)}, u32[]{:S(2)}, u32[]{:S(2)}) %all-to-all-start.2) | async-done | bytes 2097184 | tf_op jit(solution)/shard_map/all_to_all | solution.py:96
  321.4 2.3 convolution_convert_fusion
  (67 shorter events, 23.4 us)
Async XLA Ops:
  0.6 28.2 %copy-start = (bf16[6528,128]{1,0:T(8,128)(2,1)S(1)}, bf16[6528,128]{1,0:T(8,128)(2,1)}, u32[]{:S(2)}) copy-start(bf16[6528,128]{1,0:T(8,128)(2,1)} %param.17) | copy-start | bytes 5013508
  0.6 26.7 %copy-start.9 = (s32[1,19]{1,0:T(1,128)S(1)}, s32[1,19]{1,0:T(1,128)}, u32[]{:S(2)}) copy-start(s32[1,19]{1,0:T(1,128)} %param.18) | copy-start | bytes 232
  0.7 26.7 %copy-start.3 = (bf16[6528,128]{1,0:T(8,128)(2,1)S(1)}, bf16[6528,128]{1,0:T(8,128)(2,1)}, u32[]{:S(2)}) copy-start(bf16[6528,128]{1,0:T(8,128)(2,1)} %param.16) | copy-start | bytes 5013508
  2.4 0.6 copy-start.5
  4.4 26.0 %copy-start.2 = (bf16[24,1024]{1,0:T(8,128)(2,1)S(1)}, bf16[24,1024]{1,0:T(8,128)(2,1)}, u32[]{:S(2)}) copy-start(bf16[24,1024]{1,0:T(8,128)(2,1)} %param.15) | copy-start | bytes 147460
  5.1 32.5 %all-to-all-start.1 = ((bf16[64,1,1]{2,1,0:T(2,128)(2,1)}), bf16[64,1,1]{2,1,0:T(2,128)(2,1)S(1)}, u32[]{:S(2)}, u32[]{:S(2)}) async-start(bf16[64,1,1]{2,1,0:T(2,128)(2,1)} %copy.37), calls=%async_computation.1 | async-start | bytes 65536 | tf_op jit(solution)/shard_map/all_to_all | solution.py:98
  37.7 49.7 %all-to-all-start.4 = ((bf16[64,2,512]{2,1,0:T(2,128)(2,1)}), bf16[64,2,512]{2,1,0:T(2,128)(2,1)S(1)}, u32[]{:S(2)}, u32[]{:S(2)}) async-start(bf16[64,2,512]{2,1,0:T(2,128)(2,1)} %reshape.354), calls=%async_computation.4 | async-start | bytes 262144 | tf_op jit(solution)/shard_map/all_to_all | solution.py:97
  53.9 1.2 copy-start.4
  61.9 1.2 copy-start.4
  69.9 1.2 copy-start.4
  77.9 1.2 copy-start.4
  81.4 11.8 %copy-start.1 = (s32[24]{0:T(128)S(1)}, s32[24]{0:T(128)}, u32[]{:S(2)}) copy-start(s32[24]{0:T(128)} %param.21) | copy-start | bytes 292
  87.4 18.2 %all-to-all-start = ((bf16[8,48,1024]{2,1,0:T(8,128)(2,1)}), bf16[8,48,1024]{2,1,0:T(8,128)(2,1)}, u32[]{:S(2)}, u32[]{:S(2)}) async-start(bf16[8,48,1024]{2,1,0:T(8,128)(2,1)} %all_to_all.30), calls=%async_computation | async-start | bytes 1572864 | tf_op jit(solution)/shard_map/all_to_all | solution.py:76
  105.6 106.7 %all-to-all-start.3 = ((bf16[64,128,128]{2,1,0:T(8,128)(2,1)}), bf16[64,128,128]{2,1,0:T(8,128)(2,1)}, u32[]{:S(2)}, u32[]{:S(2)}) async-start(bf16[64,128,128]{2,1,0:T(8,128)(2,1)} %gather_fusion.7), calls=%async_computation.3 | async-start | bytes 4194304 | tf_op jit(solution)/shard_map/all_to_all | solution.py:95
  123.0 103.5 %copy-start.7 = (s32[2,4]{1,0:T(2,128)S(1)}, s32[2,4]{1,0:T(2,128)}, u32[]{:S(2)}) copy-start(s32[2,4]{1,0:T(2,128)} %param.19) | copy-start | bytes 100
  123.0 106.2 %copy-start.8 = (s32[2]{0:T(128)S(1)}, s32[2]{0:T(128)}, u32[]{:S(2)}) copy-start(s32[2]{0:T(128)} %param.20) | copy-start | bytes 28
  123.0 106.3 %copy-start.6 = (bf16[2,1024]{1,0:T(2,128)(2,1)S(1)}, bf16[2,1024]{1,0:T(2,128)(2,1)}, u32[]{:S(2)}) copy-start(bf16[2,1024]{1,0:T(2,128)(2,1)} %param.14) | copy-start | bytes 12292
  212.3 109.1 %all-to-all-start.2 = ((bf16[64,128,128]{2,1,0:T(8,128)(2,1)}), bf16[64,128,128]{2,1,0:T(8,128)(2,1)}, u32[]{:S(2)}, u32[]{:S(2)}) async-start(bf16[64,128,128]{2,1,0:T(8,128)(2,1)} %gather_fusion.6), calls=%async_computation.2 | async-start | bytes 4194304 | tf_op jit(solution)/shard_map/all_to_all | solution.py:96
where the time goes:
time: 328 us; the launch traced here: 324 us
  waiting for transfers between devices  183 us (56%)
  starting transfers between devices  66.2 us (20%)
  matrix products  29.8 us (9%)
  local copies, waits for them, and re-layouts  27.7 us (8%)
  other arithmetic  16.6 us (5%)
    all_to_all x1, waiting for transfers between devices, per_device(): lax.all_to_all(send_keys, 'replica', split_axis=0, concat_axis=0, tiled=T...  89.3 us
    all_to_all x1, waiting for transfers between devices, per_device(): lax.all_to_all(send_values, 'replica', split_axis=0, concat_axis=0, tiled...  81.6 us
    all_to_all x1, starting transfers between devices, per_device(): lax.all_to_all(send_len, 'replica', split_axis=0, concat_axis=0, tiled=True)  19.3 us
    dot_general x6, matrix products, score_block(): jnp.einsum('bngqd,blgd->bgqnl', queries, key_rows, preferred_element_type...  17.1 us
    all_to_all x1, starting transfers between devices, per_device(): lax.all_to_all(send_keys, 'replica', split_axis=0, concat_axis=0, tiled=T...  15.3 us
    all_to_all x1, starting transfers between devices, per_device(): lax.all_to_all(send_values, 'replica', split_axis=0, concat_axis=0, tiled...  14.2 us
    dot_general x6, matrix products, score_block(): jnp.einsum('bgqnl,blgd->bngqd', weights, value_rows, preferred_element_ty...  12.7 us
    all_to_all x1, starting transfers between devices, per_device(): lax.all_to_all(send_q, 'replica', split_axis=0, concat_axis=0, tiled=True)  11.6 us
  transfers between devices with their start and end apart: 5, of which 4 were waited for; matrix products, arithmetic and copies ran while one was open for 20% of the time, Pallas kernels for 0%

commit v1 on v0

v1 whole, which is shorter than its diff:
```python
import functools
import math

import jax
import jax.numpy as jnp
from jax import lax
from jax.experimental import pallas as pl
from jax.experimental.pallas import tpu as pltpu
from jax.sharding import PartitionSpec as P

D = 128
PAGE = 128
GROUP = 8
SCALE = math.log2(math.e) / math.sqrt(D)
NEG = -1e30
CHUNK = 1024
MESH = pl.DeviceIdType.MESH
BF16 = jnp.bfloat16
F32 = jnp.float32


def tiles(x):
    return [x[:, i : i + 128] for i in range(0, x.shape[1], 128)]


def dot_t(a, b):
    return lax.dot_general(a, b, (((1,), (1,)), ((), ())), preferred_element_type=F32)


def iota(shape, axis):
    return lax.broadcasted_iota(jnp.int32, shape, axis)


def kernel(
    sizes,
    prefill_pages,
    decode_pages,
    decode_len,
    overflow_pages,
    overflow_len,
    overflow_dest,
    prefill_q,
    decode_q,
    overflow_q,
    key_pool,
    value_pool,
    prefill_out,
    decode_out,
    moved_out,
    keys,
    values,
    queries,
    small_q,
    small_rows,
    key_rows,
    value_rows,
    score_a,
    score_b,
    blocks,
    send_rows,
    got_rows,
    wide_rows,
    in_sem,
    block_send,
    block_recv,
    own_sem,
    row_send,
    row_recv,
):
    n_rep, n_ten = sizes
    me_r, me_t = lax.axis_index("replica"), lax.axis_index("tensor")
    span = key_rows.shape[0]
    tokens = queries.shape[0]
    part = tokens // n_ten
    pair = 2 * part
    rows = pair * GROUP
    prior = span - tokens
    chips = n_ten // 2

    loads = [
        pltpu.make_async_copy(source, target, in_sem.at[i])
        for i, (source, target) in enumerate(
            (
                (overflow_q, small_q),
                (key_pool, keys),
                (value_pool, values),
                (prefill_q, queries),
            )
        )
    ]
    for load in loads:
        load.start()

    barrier = pltpu.get_barrier_semaphore()

    def greet_replica(i, _):
        pl.semaphore_signal(
            barrier, inc=1, device_id={"replica": lax.rem(me_r + i, n_rep)}, device_id_type=MESH
        )
        return 0

    def greet_tensor(i, _):
        pl.semaphore_signal(
            barrier, inc=1, device_id={"tensor": lax.rem(me_t + i, n_ten)}, device_id_type=MESH
        )
        return 0

    lax.fori_loop(1, n_rep, greet_replica, 0)
    lax.fori_loop(1, n_ten, greet_tensor, 0)

    loads[0].wait()
    n_over = overflow_q.shape[0]
    n_dec = decode_q.shape[0]
    small_rows[0:n_over, :] = small_q[...].astype(F32)
    small_rows[n_over:, :] = jnp.zeros((8, GROUP * D), F32)
    small_rows[n_over : n_over + n_dec, :] = decode_q[...].astype(F32)
    loads[1].wait()
    loads[2].wait()

    row_slot = iota((64, 128), 0) % 8
    lane = iota((64, 128), 1)
    dec_pages = decode_pages.shape[1]
    attended = []
    for g in range(n_over // 8 + 1):
        q = jnp.concatenate(
            [small_rows[g * 8 : (g + 1) * 8, h * D : (h + 1) * D] for h in range(GROUP)], axis=0
        ).astype(BF16)
        pages, owner, limit = [], [], []
        for i in range(8):
            if g < n_over // 8:
                pages.append(overflow_pages[g * 8 + i])
                owner.append(i)
                limit.append(overflow_len[g * 8 + i])
            else:
                pages.append(decode_pages[i // dec_pages, i % dec_pages])
                owner.append(i // dec_pages)
                limit.append(decode_len[i // dec_pages] - (i % dec_pages) * PAGE)
        k = jnp.concatenate([keys[p] for p in pages], axis=0)
        v = jnp.concatenate([values[p] for p in pages], axis=0)
        s = tiles(dot_t(q, k))
        s = [
            jnp.where((row_slot == owner[i]) & (lane < limit[i]), s[i] * SCALE, NEG)
            for i in range(8)
        ]
        m = jnp.max(functools.reduce(jnp.maximum, s), axis=1, keepdims=True)
        p = [jnp.exp2(x - m) for x in s]
        total = jnp.sum(functools.reduce(jnp.add, p), axis=1, keepdims=True)
        o = jnp.dot(
            jnp.concatenate([x.astype(BF16) for x in p], axis=1), v, preferred_element_type=F32
        )
        attended.append((o / total).astype(BF16))
    last = attended[-1].astype(F32)
    for h in range(GROUP):
        decode_out[:, h * D : (h + 1) * D] = last[h * 8 : h * 8 + n_dec, :].astype(BF16)

    width = 64 * (n_over // 8)
    column = iota((1, width), 1)
    request = (column // 64) * 8 + column % 8
    dest = jnp.full((1, width), -1, jnp.int32)
    for j in range(n_over):
        dest = jnp.where(request == j, overflow_dest[j], dest)
    target = iota((n_rep * 8, width), 0)
    pick = (dest * 8 + (column // 8) % 8 == target).astype(F32).astype(BF16)
    sent = jnp.dot(pick, jnp.concatenate(attended[:-1], axis=0), preferred_element_type=F32)
    send_rows[...] = sent.reshape(n_rep, 8, D).astype(BF16)
    got_rows[me_r] = send_rows[me_r]

    pl.semaphore_wait(barrier, n_rep + n_ten - 2)

    def send_row(i, _):
        to = lax.rem(me_r + i, n_rep)
        pltpu.make_async_remote_copy(
            src_ref=send_rows.at[to],
            dst_ref=got_rows.at[me_r],
            send_sem=row_send,
            recv_sem=row_recv,
            device_id={"replica": to},
            device_id_type=MESH,
        ).start()
        return 0

    lax.fori_loop(1, n_rep, send_row, 0)

    def gather(i, _):
        at = pl.ds(pl.multiple_of(i * PAGE, PAGE), PAGE)
        listed = prefill_pages[0, i]
        page = keys[listed]
        key_rows[at, 0:D] = page
        key_rows[at, D : 2 * D] = page
        value_rows[at, 0:D] = values[listed]
        value_rows[at, D : 2 * D] = jnp.ones((PAGE, D), BF16)
        return 0

    lax.fori_loop(0, span // PAGE, gather, 0)
    loads[3].wait()

    chunks = [(o, min(CHUNK, span - o)) for o in range(0, span, CHUNK)]
    scratch = (score_a, score_b)
    me_x = me_t // 2

    def block_copy(at, to):
        offset = pl.multiple_of((to % 2) * part, 16)
        return pltpu.make_async_remote_copy(
            src_ref=blocks.at[at, pl.ds(offset, part), :],
            dst_ref=prefill_out.at[:, pl.ds(pl.multiple_of(me_t * GROUP * D, GROUP * D), GROUP * D)],
            send_sem=block_send.at[to],
            recv_sem=block_recv.at[me_t],
            device_id={"tensor": to},
            device_id_type=MESH,
        )

    def block(step, _):
        ahead = jnp.where(step < 2, 2 - step, 9 - 3 * step)
        chip = lax.rem(me_x + ahead, chips)
        at = pl.ds(pl.multiple_of(chip * pair, pair), pair)
        q = jnp.concatenate([queries[at, h * D : (h + 1) * D] for h in range(GROUP)], axis=0)
        q = q.astype(F32) * SCALE
        high = q.astype(BF16)
        q = jnp.concatenate([high, (q - high.astype(F32)).astype(BF16)], axis=1)
        peak = [None] * len(chunks)

        def scores(j):
            o, w = chunks[j]
            s = dot_t(q, key_rows[o : o + w, :])
            if o + w > prior:
                token = iota((rows, w), 0) % pair + chip * pair
                s = jnp.where(iota((rows, w), 1) + (o - prior) <= token, s, NEG)
            m = jnp.max(functools.reduce(jnp.maximum, tiles(s)), axis=1, keepdims=True)
            m = jnp.broadcast_to(m, (rows, 128))
            peak[j] = m if j == 0 else jnp.maximum(peak[j - 1], m)
            scratch[j % 2][:, :w] = s

        def weigh(j, acc):
            o, w = chunks[j]
            p = [jnp.exp2(x - peak[j]).astype(BF16) for x in tiles(scratch[j % 2][:, :w])]
            o = jnp.dot(
                jnp.concatenate(p, axis=1), value_rows[o : o + w, :], preferred_element_type=F32
            )
            if acc is None:
                return o
            shrink = jnp.exp2(peak[j - 1] - peak[j])
            return jnp.concatenate([x * shrink for x in tiles(acc)], axis=1) + o

        acc = None
        for j in range(len(chunks) + 1):
            if j < len(chunks):
                scores(j)
            if j > 0:
                acc = weigh(j - 1, acc)
        out = (acc[:, :D] / acc[:, D:]).astype(BF16)
        for h in range(GROUP):
            blocks[step, :, h * D : (h + 1) * D] = out[h * pair : (h + 1) * pair, :]

        for core in range(2):
            to = chip * 2 + core

            @pl.when(to != me_t)
            def _():
                block_copy(step, to).start()

        return 0

    lax.fori_loop(0, chips, block, 0)

    own = pltpu.make_async_copy(
        blocks.at[chips - 1, pl.ds(pl.multiple_of((me_t % 2) * part, 16), part), :],
        prefill_out.at[:, pl.ds(pl.multiple_of(me_t * GROUP * D, GROUP * D), GROUP * D)],
        own_sem,
    )
    own.start()

    pltpu.make_async_copy(got_rows.at[0 : n_rep - 1], got_rows.at[0 : n_rep - 1], row_recv).wait()
    pltpu.make_async_copy(send_rows.at[0 : n_rep - 1], send_rows.at[0 : n_rep - 1], row_send).wait()
    wide_rows[...] = got_rows[...].astype(F32).reshape(n_rep * 8, D)
    for h in range(GROUP):
        moved_out[:, h * D : (h + 1) * D] = wide_rows[pl.ds(h, n_rep, stride=8), :].astype(BF16)

    own.wait()

    def finish(i, _):
        other = lax.rem(me_t + i, n_ten)
        arrived = prefill_out.at[
            :, pl.ds(pl.multiple_of(other * GROUP * D, GROUP * D), GROUP * D)
        ]
        pltpu.make_async_copy(arrived, arrived, block_recv.at[other]).wait()
        left = blocks.at[0, 0:part, :]
        pltpu.make_async_copy(left, left, block_send.at[other]).wait()
        return 0

    lax.fori_loop(1, n_ten, finish, 0)


def per_device(
    prefill_q,
    decode_q,
    overflow_q,
    key_pool,
    value_pool,
    prefill_pages,
    decode_pages,
    decode_len,
    overflow_pages,
    overflow_len,
    overflow_dest,
):
    n_rep, n_ten = lax.axis_size("replica"), lax.axis_size("tensor")
    tokens, width = prefill_q.shape
    span = prefill_pages.shape[1] * PAGE
    rows = 2 * tokens // n_ten * GROUP
    n_over = overflow_q.shape[0]
    key_pool = key_pool.reshape(-1, PAGE, D)
    value_pool = value_pool.reshape(-1, PAGE, D)
    smem = pl.BlockSpec(memory_space=pltpu.SMEM)
    vmem = pl.BlockSpec(memory_space=pltpu.VMEM)
    hbm = pl.BlockSpec(memory_space=pl.ANY)
    return pl.pallas_call(
        functools.partial(kernel, (n_rep, n_ten)),
        out_shape=(
            jax.ShapeDtypeStruct((tokens // n_ten, width * n_ten), BF16),
            jax.ShapeDtypeStruct(decode_q.shape, BF16),
            jax.ShapeDtypeStruct((n_rep, width), BF16),
        ),
        in_specs=[smem] * 6 + [hbm, vmem, hbm, hbm, hbm],
        out_specs=(hbm, vmem, vmem),
        scratch_shapes=[
            pltpu.VMEM(key_pool.shape, BF16),
            pltpu.VMEM(key_pool.shape, BF16),
            pltpu.VMEM((tokens, width), BF16),
            pltpu.VMEM((n_over, width), BF16),
            pltpu.VMEM((n_over + 8, width), F32),
            pltpu.VMEM((span, 2 * D), BF16),
            pltpu.VMEM((span, 2 * D), BF16),
            pltpu.VMEM((rows, CHUNK), F32),
            pltpu.VMEM((rows, CHUNK), F32),
            pltpu.VMEM((n_ten // 2, 2 * tokens // n_ten, width), BF16),
            pltpu.VMEM((n_rep, 8, D), BF16),
            pltpu.VMEM((n_rep, 8, D), BF16),
            pltpu.VMEM((n_rep * 8, D), F32),
            pltpu.SemaphoreType.DMA((4,)),
            pltpu.SemaphoreType.DMA((n_ten,)),
            pltpu.SemaphoreType.DMA((n_ten,)),
            pltpu.SemaphoreType.DMA,
            pltpu.SemaphoreType.DMA,
            pltpu.SemaphoreType.DMA,
        ],
        compiler_params=pltpu.CompilerParams(
            collective_id=0, has_side_effects=True, vmem_limit_bytes=56 << 20
        ),
    )(
        prefill_pages,
        decode_pages,
        decode_len,
        overflow_pages,
        overflow_len,
        overflow_dest,
        prefill_q,
        decode_q,
        overflow_q,
        key_pool,
        value_pool,
    )


def solution(mesh):
    both = P("replica", "tensor")
    in_specs = (both,) * 5 + (P("replica", None),) * 2 + (P("replica"),) * 4
    out_specs = (P(("replica", "tensor"), None), both, both)
    return jax.shard_map(
        per_device, mesh=mesh, in_specs=in_specs, out_specs=out_specs, check_vma=False
    )
```

time: 328 us -> 40.2 us (0.12); the launches traced: 324 us -> 40 us
  waiting for transfers between devices: 183 us -> 0 us
  starting transfers between devices: 66.2 us -> 0 us
  Pallas kernels: 0 us -> 35.4 us
  matrix products: 29.8 us -> 0 us
  local copies, waits for them, and re-layouts: 27.7 us -> 4.03 us
  other arithmetic: 16.6 us -> 0 us
    all_to_all x5 -> x0, waiting for transfers between devices: 183 us -> none  [the longest x1 89.3 us: per_device(): lax.all_to_all(send_keys, 'replica', split_axis=0, concat_axis=0, tiled=T...]
    all_to_all x5 -> x0, starting transfers between devices: 66.2 us -> none  [the longest x1 19.3 us: per_device(): lax.all_to_all(send_len, 'replica', split_axis=0, concat_axis=0, tiled=True)]
    pallas_call x0 -> x1, Pallas kernels: none -> 35.4 us  [per_device(): pl.pallas_call(functools.partial(kernel, (n_rep, n_ten)), out_shape=(jax....]
    dot_general x12 -> x0, matrix products: 29.8 us -> none  [the longest x6 17.1 us: score_block(): jnp.einsum('bngqd,blgd->bgqnl', queries, key_rows, preferred_element_type...]
    gather x9 -> x0, local copies, waits for them, and re-layouts: 13 us -> none  [the longest x1 2.15 us: per_device(): send_keys = key_pages[send_pages]]
    reduce_sum x7 -> x0, other arithmetic: 5.89 us -> none  [the longest x6 4.99 us: score_block(): jnp.sum(expon, axis=-1, keepdims=True)]
    all_to_all x3 -> x0, local copies, waits for them, and re-layouts: 5.78 us -> none  [the longest x2 5.21 us: per_device(): lax.all_to_all(local_heads, 'tensor', split_axis=0, concat_axis=1, tiled=...]
    le x4 -> x0, other arithmetic: 5.08 us -> none  [prefill_heads(): jnp.arange(key_span)[None, :] <= earlier + jnp.arange(tokens)[:, None]]
  transfers between devices with their start and end apart: 5 -> 0, of which waited for: 4 -> 0; matrix products, arithmetic and copies ran while one was open for 20% -> 0% of each run, Pallas kernels for 0% -> 0%
where the time goes in v1:
time: 40.2 us; the launch traced here: 40 us
  Pallas kernels  35.4 us (88%)
  local copies, waits for them, and re-layouts  4.03 us (10%)
  between operations  0.65 us (2%)
    pallas_call x1, Pallas kernels, per_device(): pl.pallas_call(functools.partial(kernel, (n_rep, n_ten)), out_shape=(jax....  35.4 us
    unnamed x5, local copies, waits for them, and re-layouts  4.03 us

profile of v1, /device:TPU:1, one launch (start us, length us, event | category | flops | bytes accessed | tf_op | source)
XLA Modules:
  0.0 40.0 jit_solution(11165117285766404214)
XLA Ops:
  0.6 35.4 %shard_map.130 = (bf16[48,8192]{1,0:T(8,128)(2,1)}, bf16[2,1024]{1,0:T(2,128)(2,1)}, bf16[64,1024]{1,0:T(8,128)(2,1)}) custom-call(s32[1,19]{1,0:T(1,128)} %prefill_pages.1, s32[2,4]{1,0:T(2,128)} %decode_pages.1, s32[2]{0:T(128)} %decode_len.1, s32[24]{0:T(128)} %overflow_pages.1, s32[24]{0:T(128)} %overflow_len.1, s32[24]{0:T(128)} %overflow_dest.1, ...), custom_call_target="tpu_custom_call" | custom-call | tf_op jit(solution)/shard_map/pallas_call | solution.py:316
  36.0 0.0 copy-start
  36.0 2.1 %copy.17 = bf16[48,8192]{1,0:T(8,128)(2,1)} copy(bf16[48,8192]{1,0:T(8,128)(2,1)} %get-tuple-element.6) | data formatting | bytes 1572864
  38.1 1.3 %copy.18 = bf16[2,1024]{1,0:T(2,128)(2,1)} copy(bf16[2,1024]{1,0:T(2,128)(2,1)} %get-tuple-element.7) | data formatting | bytes 8192
  39.4 0.0 copy-done
  39.4 0.7 %copy.19 = bf16[64,1024]{1,0:T(8,128)(2,1)} copy(bf16[64,1024]{1,0:T(8,128)(2,1)S(1)} %copy-done) | data formatting | bytes 262144
Async XLA Ops:
  36.0 3.4 %copy-start = (bf16[64,1024]{1,0:T(8,128)(2,1)S(1)}, bf16[64,1024]{1,0:T(8,128)(2,1)}, u32[]{:S(2)}) copy-start(bf16[64,1024]{1,0:T(8,128)(2,1)} %get-tuple-element.8) | copy-start | bytes 393220

commit v2 on v1

--- a/solution.py
+++ b/solution.py
@@ -14,6 +14,8 @@
 SCALE = math.log2(math.e) / math.sqrt(D)
 NEG = -1e30
 CHUNK = 1024
+ATTEND_VMEM = 24 << 20
+PLACE_VMEM = 8 << 20
 MESH = pl.DeviceIdType.MESH
 BF16 = jnp.bfloat16
 F32 = jnp.float32
@@ -33,12 +35,12 @@
 
 def kernel(
     sizes,
-    prefill_pages,
-    decode_pages,
-    decode_len,
-    overflow_pages,
-    overflow_len,
-    overflow_dest,
+    prefill_pages_hbm,
+    decode_pages_hbm,
+    decode_len_hbm,
+    overflow_pages_hbm,
+    overflow_len_hbm,
+    overflow_dest_hbm,
     prefill_q,
     decode_q,
     overflow_q,
@@ -46,7 +48,14 @@
     value_pool,
     prefill_out,
     decode_out,
-    moved_out,
+    moved_rows,
+    prefill_pages,
+    decode_pages,
+    decode_len,
+    overflow_pages,
+    overflow_len,
+    overflow_dest,
+    decode_held,
     keys,
     values,
     queries,
@@ -58,16 +67,16 @@
     score_b,
     blocks,
     send_rows,
-    got_rows,
-    wide_rows,
+    table_sem,
     in_sem,
     block_send,
     block_recv,
     own_sem,
+    kept_sem,
     row_send,
     row_recv,
 ):
-    n_rep, n_ten = sizes
+    n_rep, n_ten, depth_z = sizes
     me_r, me_t = lax.axis_index("replica"), lax.axis_index("tensor")
     span = key_rows.shape[0]
     tokens = queries.shape[0]
@@ -77,6 +86,20 @@
     prior = span - tokens
     chips = n_ten // 2
 
+    tables = [
+        pltpu.make_async_copy(source, target, table_sem.at[i])
+        for i, (source, target) in enumerate(
+            (
+                (prefill_pages_hbm, prefill_pages),
+                (decode_pages_hbm, decode_pages),
+                (decode_len_hbm, decode_len),
+                (overflow_pages_hbm, overflow_pages),
+                (overflow_len_hbm, overflow_len),
+                (overflow_dest_hbm, overflow_dest),
+                (decode_q, decode_held),
+            )
+        )
+    ]
     loads = [
         pltpu.make_async_copy(source, target, in_sem.at[i])
         for i, (source, target) in enumerate(
@@ -88,7 +111,7 @@
             )
         )
     ]
-    for load in loads:
+    for load in loads + tables:
         load.start()
 
     barrier = pltpu.get_barrier_semaphore()
@@ -108,12 +131,14 @@
     lax.fori_loop(1, n_rep, greet_replica, 0)
     lax.fori_loop(1, n_ten, greet_tensor, 0)
 
+    for table in tables:
+        table.wait()
     loads[0].wait()
     n_over = overflow_q.shape[0]
     n_dec = decode_q.shape[0]
     small_rows[0:n_over, :] = small_q[...].astype(F32)
     small_rows[n_over:, :] = jnp.zeros((8, GROUP * D), F32)
-    small_rows[n_over : n_over + n_dec, :] = decode_q[...].astype(F32)
+    small_rows[n_over : n_over + n_dec, :] = decode_held[...].astype(F32)
     loads[1].wait()
     loads[2].wait()
 
@@ -163,23 +188,20 @@
     pick = (dest * 8 + (column // 8) % 8 == target).astype(F32).astype(BF16)
     sent = jnp.dot(pick, jnp.concatenate(attended[:-1], axis=0), preferred_element_type=F32)
     send_rows[...] = sent.reshape(n_rep, 8, D).astype(BF16)
-    got_rows[me_r] = send_rows[me_r]
-
-    pl.semaphore_wait(barrier, n_rep + n_ten - 2)
+    kept = pltpu.make_async_copy(send_rows.at[me_r], moved_rows.at[me_r], kept_sem)
+    kept.start()
 
     def send_row(i, _):
         to = lax.rem(me_r + i, n_rep)
         pltpu.make_async_remote_copy(
             src_ref=send_rows.at[to],
-            dst_ref=got_rows.at[me_r],
+            dst_ref=moved_rows.at[me_r],
             send_sem=row_send,
             recv_sem=row_recv,
             device_id={"replica": to},
             device_id_type=MESH,
         ).start()
         return 0
-
-    lax.fori_loop(1, n_rep, send_row, 0)
 
     def gather(i, _):
         at = pl.ds(pl.multiple_of(i * PAGE, PAGE), PAGE)
@@ -209,9 +231,33 @@
             device_id_type=MESH,
         )
 
+    def chip_of(step):
+        return lax.rem(me_x + jnp.where(step < 2, 2 - step, 9 - 3 * step), chips)
+
+    def send_block(step):
+        for core in range(2):
+            to = chip_of(step) * 2 + core
+
+            @pl.when(to != me_t)
+            def _():
+                block_copy(step, to).start()
+
+    z = lax.rem(me_r, depth_z)
+    hold = jnp.where(z < 4, 3, jnp.where(z < 8, 1, 0))
+
     def block(step, _):
-        ahead = jnp.where(step < 2, 2 - step, 9 - 3 * step)
-        chip = lax.rem(me_x + ahead, chips)
+        @pl.when(step == hold)
+        def _():
+            pl.semaphore_wait(barrier, n_rep + n_ten - 2)
+            lax.fori_loop(1, n_rep, send_row, 0)
+
+            def send_held(i, _):
+                send_block(i)
+                return 0
+
+            lax.fori_loop(0, step, send_held, 0)
+
+        chip = chip_of(step)
         at = pl.ds(pl.multiple_of(chip * pair, pair), pair)
         q = jnp.concatenate([queries[at, h * D : (h + 1) * D] for h in range(GROUP)], axis=0)
         q = q.astype(F32) * SCALE
@@ -251,12 +297,9 @@
         for h in range(GROUP):
             blocks[step, :, h * D : (h + 1) * D] = out[h * pair : (h + 1) * pair, :]
 
-        for core in range(2):
-            to = chip * 2 + core
-
-            @pl.when(to != me_t)
-            def _():
-                block_copy(step, to).start()
+        @pl.when(step >= hold)
+        def _():
+            send_block(step)
 
         return 0
 
@@ -269,12 +312,10 @@
     )
     own.start()
 
-    pltpu.make_async_copy(got_rows.at[0 : n_rep - 1], got_rows.at[0 : n_rep - 1], row_recv).wait()
+    kept.wait()
+    rest = moved_rows.at[0 : n_rep - 1]
+    pltpu.make_async_copy(rest, rest, row_recv).wait()
     pltpu.make_async_copy(send_rows.at[0 : n_rep - 1], send_rows.at[0 : n_rep - 1], row_send).wait()
-    wide_rows[...] = got_rows[...].astype(F32).reshape(n_rep * 8, D)
-    for h in range(GROUP):
-        moved_out[:, h * D : (h + 1) * D] = wide_rows[pl.ds(h, n_rep, stride=8), :].astype(BF16)
-
     own.wait()
 
     def finish(i, _):
@@ -288,6 +329,43 @@
         return 0
 
     lax.fori_loop(1, n_ten, finish, 0)
+
+
+def place_kernel(prefill, decode, moved, prefill_out, decode_out, moved_out, wide, flat, sem):
+    n = moved.shape[0]
+    writes = [
+        pltpu.make_async_copy(prefill, prefill_out, sem.at[0]),
+        pltpu.make_async_copy(decode, decode_out, sem.at[1]),
+        pltpu.make_async_copy(flat, moved_out, sem.at[2]),
+    ]
+    writes[0].start()
+    writes[1].start()
+    wide[...] = moved[...].astype(F32).reshape(n * 8, D)
+    for h in range(GROUP):
+        flat[:, h * D : (h + 1) * D] = wide[pl.ds(h, n, stride=8), :].astype(BF16)
+    writes[2].start()
+    for write in writes:
+        write.wait()
+
+
+def place(prefill, decode, moved):
+    n = moved.shape[0]
+    return pl.pallas_call(
+        place_kernel,
+        out_shape=(
+            jax.ShapeDtypeStruct(prefill.shape, BF16),
+            jax.ShapeDtypeStruct(decode.shape, BF16),
+            jax.ShapeDtypeStruct((n, GROUP * D), BF16),
+        ),
+        in_specs=[pl.BlockSpec(memory_space=pltpu.VMEM)] * 3,
+        out_specs=(pl.BlockSpec(memory_space=pltpu.HBM),) * 3,
+        scratch_shapes=[
+            pltpu.VMEM((n * 8, D), F32),
+            pltpu.VMEM((n, GROUP * D), BF16),
+            pltpu.SemaphoreType.DMA((3,)),
+        ],
+        compiler_params=pltpu.CompilerParams(vmem_limit_bytes=PLACE_VMEM),
+    )(prefill, decode, moved)
 
 
 def per_device(
@@ -310,19 +388,26 @@
     n_over = overflow_q.shape[0]
     key_pool = key_pool.reshape(-1, PAGE, D)
     value_pool = value_pool.reshape(-1, PAGE, D)
-    smem = pl.BlockSpec(memory_space=pltpu.SMEM)
     vmem = pl.BlockSpec(memory_space=pltpu.VMEM)
-    hbm = pl.BlockSpec(memory_space=pl.ANY)
-    return pl.pallas_call(
-        functools.partial(kernel, (n_rep, n_ten)),
+    hbm = pl.BlockSpec(memory_space=pltpu.HBM)
+    free = pl.BlockSpec(memory_space=pl.ANY)
+    raw = pl.pallas_call(
+        functools.partial(kernel, (n_rep, n_ten, 16)),
         out_shape=(
             jax.ShapeDtypeStruct((tokens // n_ten, width * n_ten), BF16),
             jax.ShapeDtypeStruct(decode_q.shape, BF16),
-            jax.ShapeDtypeStruct((n_rep, width), BF16),
+            jax.ShapeDtypeStruct((n_rep, 8, D), BF16),
         ),
-        in_specs=[smem] * 6 + [hbm, vmem, hbm, hbm, hbm],
-        out_specs=(hbm, vmem, vmem),
+        in_specs=[hbm] * 11,
+        out_specs=(free, vmem, free),
         scratch_shapes=[
+            pltpu.SMEM(prefill_pages.shape, jnp.int32),
+            pltpu.SMEM(decode_pages.shape, jnp.int32),
+            pltpu.SMEM(decode_len.shape, jnp.int32),
+            pltpu.SMEM(overflow_pages.shape, jnp.int32),
+            pltpu.SMEM(overflow_len.shape, jnp.int32),
+            pltpu.SMEM(overflow_dest.shape, jnp.int32),
+            pltpu.VMEM(decode_q.shape, BF16),
             pltpu.VMEM(key_pool.shape, BF16),
             pltpu.VMEM(key_pool.shape, BF16),
             pltpu.VMEM((tokens, width), BF16),
@@ -334,31 +419,37 @@
             pltpu.VMEM((rows, CHUNK), F32),
             pltpu.VMEM((n_ten // 2, 2 * tokens // n_ten, width), BF16),
             pltpu.VMEM((n_rep, 8, D), BF16),
-            pltpu.VMEM((n_rep, 8, D), BF16),
-            pltpu.VMEM((n_rep * 8, D), F32),
+            pltpu.SemaphoreType.DMA((7,)),
             pltpu.SemaphoreType.DMA((4,)),
             pltpu.SemaphoreType.DMA((n_ten,)),
             pltpu.SemaphoreType.DMA((n_ten,)),
             pltpu.SemaphoreType.DMA,
             pltpu.SemaphoreType.DMA,
             pltpu.SemaphoreType.DMA,
+            pltpu.SemaphoreType.DMA,
         ],
         compiler_params=pltpu.CompilerParams(
-            collective_id=0, has_side_effects=True, vmem_limit_bytes=56 << 20
+            collective_id=0, has_side_effects=True, vmem_limit_bytes=ATTEND_VMEM
         ),
     )(
-        prefill_pages,
-        decode_pages,
-        decode_len,
-        overflow_pages,
-        overflow_len,
-        overflow_dest,
-        prefill_q,
-        decode_q,
-        overflow_q,
-        key_pool,
-        value_pool,
+        *(
+            pltpu.with_memory_space_constraint(x, pltpu.HBM)
+            for x in (
+                prefill_pages,
+                decode_pages,
+                decode_len,
+                overflow_pages,
+                overflow_len,
+                overflow_dest,
+                prefill_q,
+                decode_q,
+                overflow_q,
+                key_pool,
+                value_pool,
+            )
+        )
     )
+    return place(*raw)
 
 
 def solution(mesh):

time: 40.2 us -> 32.6 us (0.81)
  local copies, waits for them, and re-layouts: 4.03 us -> 0 us
  Pallas kernels: 35.4 us -> 31.8 us
    unnamed x5 -> x0, local copies, waits for them, and re-layouts: 4.03 us -> none
    pallas_call x1 -> x2, Pallas kernels: 35.4 us -> 31.8 us  [the longest x1 30.9 us: per_device(): pl.pallas_call(functools.partial(kernel, (n_rep, n_ten, 16)), out_shape=(...]
where the time goes in v2:
time: 32.6 us; the launch traced here: 32.5 us
  Pallas kernels  31.8 us (98%)
  between operations  0.64 us (2%)
    pallas_call x1, Pallas kernels, per_device(): pl.pallas_call(functools.partial(kernel, (n_rep, n_ten, 16)), out_shape=(...  30.9 us
    pallas_call x1, Pallas kernels, place(): pl.pallas_call(place_kernel, out_shape=(jax.ShapeDtypeStruct(prefill.shap...  0.95 us

profile of v2, /device:TPU:1, one launch (start us, length us, event | category | flops | bytes accessed | tf_op | source)
XLA Modules:
  0.0 32.5 jit_solution(740227516602120663)
XLA Ops:
  0.6 30.9 %shard_map.130 = (bf16[48,8192]{1,0:T(8,128)(2,1)S(1)}, bf16[2,1024]{1,0:T(2,128)(2,1)S(1)}, bf16[64,8,128]{2,1,0:T(8,128)(2,1)S(1)}) custom-call(s32[1,19]{1,0:T(1,128)} %prefill_pages_hbm.1, s32[2,4]{1,0:T(2,128)} %decode_pages_hbm.1, s32[2]{0:T(128)} %decode_len_hbm.1, s32[24]{0:T(128)} %overflow_pages_hbm.1, s32[24]{0:T(128)} %overflow_len_hbm.1, ...), custom_call_target="tpu_custom_call" | custom-call | tf_op jit(solution)/shard_map/pallas_call | solution.py:394
  31.5 0.9 %shard_map.131 = (bf16[48,8192]{1,0:T(8,128)(2,1)}, bf16[2,1024]{1,0:T(2,128)(2,1)}, bf16[64,1024]{1,0:T(8,128)(2,1)}) custom-call(bf16[48,8192]{1,0:T(8,128)(2,1)S(1)} %get-tuple-element.6.prefill, bf16[2,1024]{1,0:T(2,128)(2,1)S(1)} %get-tuple-element.7.decode, bf16[64,8,128]{2,1,0:T(8,128)(2,1)S(1)} %get-tuple-element.8.moved), custom_call_target="tpu_custom_call" | custom-call | tf_op jit(solution)/shard_map/pallas_call | solution.py:353

commit v3 on v2

--- a/solution.py
+++ b/solution.py
@@ -75,6 +75,8 @@
     kept_sem,
     row_send,
     row_recv,
+    everyone,
+    group,
 ):
     n_rep, n_ten, depth_z = sizes
     me_r, me_t = lax.axis_index("replica"), lax.axis_index("tensor")
@@ -111,25 +113,37 @@
             )
         )
     ]
+
+    barrier = pltpu.get_barrier_semaphore()
+
+    y, z = me_r // depth_z, lax.rem(me_r, depth_z)
+    n_y = n_rep // depth_z
+    host = n_ten - 1
+    helper = n_ten - 2
+    hosts = me_t == host
+    hold = jnp.where(z < 4, 4, jnp.where(z < 8, 2, 0))
+
+    def to_replicas(act):
+        def body(i, _):
+            to = lax.rem(y + lax.rem(i, n_y), n_y) * depth_z + i // n_y
+            pl.when(to != me_r)(lambda: act(to))
+            return 0
+
+        lax.fori_loop(0, n_rep, body, 0)
+
+    def greet_replica(to):
+        pl.semaphore_signal(
+            barrier, inc=1, device_id={"replica": to, "tensor": jnp.minimum(me_t, helper)}, device_id_type=MESH
+        )
+
+    to_replicas(greet_replica)
+
+    @pl.when(jnp.logical_not(hosts))
+    def _():
+        pl.semaphore_signal(barrier, inc=1, device_id={"tensor": host}, device_id_type=MESH)
+
     for load in loads + tables:
         load.start()
-
-    barrier = pltpu.get_barrier_semaphore()
-
-    def greet_replica(i, _):
-        pl.semaphore_signal(
-            barrier, inc=1, device_id={"replica": lax.rem(me_r + i, n_rep)}, device_id_type=MESH
-        )
-        return 0
-
-    def greet_tensor(i, _):
-        pl.semaphore_signal(
-            barrier, inc=1, device_id={"tensor": lax.rem(me_t + i, n_ten)}, device_id_type=MESH
-        )
-        return 0
-
-    lax.fori_loop(1, n_rep, greet_replica, 0)
-    lax.fori_loop(1, n_ten, greet_tensor, 0)
 
     for table in tables:
         table.wait()
@@ -191,8 +205,7 @@
     kept = pltpu.make_async_copy(send_rows.at[me_r], moved_rows.at[me_r], kept_sem)
     kept.start()
 
-    def send_row(i, _):
-        to = lax.rem(me_r + i, n_rep)
+    def send_row(to):
         pltpu.make_async_remote_copy(
             src_ref=send_rows.at[to],
             dst_ref=moved_rows.at[me_r],
@@ -201,7 +214,6 @@
             device_id={"replica": to},
             device_id_type=MESH,
         ).start()
-        return 0
 
     def gather(i, _):
         at = pl.ds(pl.multiple_of(i * PAGE, PAGE), PAGE)
@@ -242,21 +254,40 @@
             def _():
                 block_copy(step, to).start()
 
-    z = lax.rem(me_r, depth_z)
-    hold = jnp.where(z < 4, 3, jnp.where(z < 8, 1, 0))
+    def tell(i, _):
+        pl.semaphore_signal(group, inc=1, device_id={"tensor": i}, device_id_type=MESH)
+        return 0
+
+    def meet_group():
+        @pl.when(hosts)
+        def _():
+            pl.semaphore_wait(barrier, n_ten - 1)
+            lax.fori_loop(0, host, tell, 0)
+
+        @pl.when(jnp.logical_not(hosts))
+        def _():
+            pl.semaphore_wait(group, 1)
+
+    def meet():
+        @pl.when(me_t < helper)
+        def _():
+            pl.semaphore_wait(barrier, n_rep - 1)
+
+        @pl.when(me_t == helper)
+        def _():
+            pl.semaphore_wait(barrier, 2 * (n_rep - 1))
+            pl.semaphore_signal(everyone, inc=1, device_id={"tensor": host}, device_id_type=MESH)
+
+        @pl.when(hosts)
+        def _():
+            pl.semaphore_wait(everyone, 1)
+
+        to_replicas(send_row)
 
     def block(step, _):
-        @pl.when(step == hold)
-        def _():
-            pl.semaphore_wait(barrier, n_rep + n_ten - 2)
-            lax.fori_loop(1, n_rep, send_row, 0)
-
-            def send_held(i, _):
-                send_block(i)
-                return 0
-
-            lax.fori_loop(0, step, send_held, 0)
-
+        at_once = hosts | (hold == 0)
+        pl.when((step == 0) & at_once)(meet_group)
+        pl.when(step == hold)(meet)
         chip = chip_of(step)
         at = pl.ds(pl.multiple_of(chip * pair, pair), pair)
         q = jnp.concatenate([queries[at, h * D : (h + 1) * D] for h in range(GROUP)], axis=0)
@@ -297,13 +328,12 @@
         for h in range(GROUP):
             blocks[step, :, h * D : (h + 1) * D] = out[h * pair : (h + 1) * pair, :]
 
-        @pl.when(step >= hold)
-        def _():
-            send_block(step)
-
+        pl.when((step == 0) & jnp.logical_not(at_once))(meet_group)
+        send_block(step)
         return 0
 
     lax.fori_loop(0, chips, block, 0)
+    pl.when(hold == chips)(meet)
 
     own = pltpu.make_async_copy(
         blocks.at[chips - 1, pl.ds(pl.multiple_of((me_t % 2) * part, 16), part), :],
@@ -427,6 +457,8 @@
             pltpu.SemaphoreType.DMA,
             pltpu.SemaphoreType.DMA,
             pltpu.SemaphoreType.DMA,
+            pltpu.SemaphoreType.REGULAR,
+            pltpu.SemaphoreType.REGULAR,
         ],
         compiler_params=pltpu.CompilerParams(
             collective_id=0, has_side_effects=True, vmem_limit_bytes=ATTEND_VMEM

time: 32.6 us -> 29.6 us (0.908)
  the two profiles are of different devices: /device:TPU:1 before, /device:TPU:2 now
where the time goes in v3:
time: 29.6 us; the launch traced here: 29.5 us
  Pallas kernels  28.8 us (97%)
  between operations  0.64 us (2%)
    pallas_call x1, Pallas kernels, per_device(): pl.pallas_call(functools.partial(kernel, (n_rep, n_ten, 16)), out_shape=(...  27.9 us
    pallas_call x1, Pallas kernels, place(): pl.pallas_call(place_kernel, out_shape=(jax.ShapeDtypeStruct(prefill.shap...  0.95 us

profile of v3, /device:TPU:2, one launch (start us, length us, event | category | flops | bytes accessed | tf_op | source)
XLA Modules:
  0.0 29.5 jit_solution(2785693946152232216)
XLA Ops:
  0.6 27.9 %shard_map.130 = (bf16[48,8192]{1,0:T(8,128)(2,1)S(1)}, bf16[2,1024]{1,0:T(2,128)(2,1)S(1)}, bf16[64,8,128]{2,1,0:T(8,128)(2,1)S(1)}) custom-call(s32[1,19]{1,0:T(1,128)} %prefill_pages_hbm.1, s32[2,4]{1,0:T(2,128)} %decode_pages_hbm.1, s32[2]{0:T(128)} %decode_len_hbm.1, s32[24]{0:T(128)} %overflow_pages_hbm.1, s32[24]{0:T(128)} %overflow_len_hbm.1, ...), custom_call_target="tpu_custom_call" | custom-call | tf_op jit(solution)/shard_map/pallas_call | solution.py:424
  28.5 0.9 %shard_map.131 = (bf16[48,8192]{1,0:T(8,128)(2,1)}, bf16[2,1024]{1,0:T(2,128)(2,1)}, bf16[64,1024]{1,0:T(8,128)(2,1)}) custom-call(bf16[48,8192]{1,0:T(8,128)(2,1)S(1)} %get-tuple-element.6.prefill, bf16[2,1024]{1,0:T(2,128)(2,1)S(1)} %get-tuple-element.7.decode, bf16[64,8,128]{2,1,0:T(8,128)(2,1)S(1)} %get-tuple-element.8.moved), custom_call_target="tpu_custom_call" | custom-call | tf_op jit(solution)/shard_map/pallas_call | solution.py:383

commit v4 on v3

--- a/solution.py
+++ b/solution.py
@@ -114,6 +114,8 @@
         )
     ]
 
+    for load in loads + tables:
+        load.start()
     barrier = pltpu.get_barrier_semaphore()
 
     y, z = me_r // depth_z, lax.rem(me_r, depth_z)
@@ -121,7 +123,7 @@
     host = n_ten - 1
     helper = n_ten - 2
     hosts = me_t == host
-    hold = jnp.where(z < 4, 4, jnp.where(z < 8, 2, 0))
+    hold = jnp.where(z < 3, 4, jnp.where(z < 5, 3, jnp.where(z < 8, 1, 0)))
 
     def to_replicas(act):
         def body(i, _):
@@ -142,8 +144,6 @@
     def _():
         pl.semaphore_signal(barrier, inc=1, device_id={"tensor": host}, device_id_type=MESH)
 
-    for load in loads + tables:
-        load.start()
 
     for table in tables:
         table.wait()

time: 29.6 us -> 28.1 us (0.949)
  the two profiles are of different devices: /device:TPU:2 before, /device:TPU:6 now
where the time goes in v4:
time: 28.1 us; the launch traced here: 28 us
  Pallas kernels  27.3 us (97%)
  between operations  0.64 us (2%)
    pallas_call x1, Pallas kernels, per_device(): pl.pallas_call(functools.partial(kernel, (n_rep, n_ten, 16)), out_shape=(...  26.4 us
    pallas_call x1, Pallas kernels, place(): pl.pallas_call(place_kernel, out_shape=(jax.ShapeDtypeStruct(prefill.shap...  0.95 us

profile of v4, /device:TPU:6, one launch (start us, length us, event | category | flops | bytes accessed | tf_op | source)
XLA Modules:
  0.0 28.0 jit_solution(8784273549690939190)
XLA Ops:
  0.6 26.4 %shard_map.130 = (bf16[48,8192]{1,0:T(8,128)(2,1)S(1)}, bf16[2,1024]{1,0:T(2,128)(2,1)S(1)}, bf16[64,8,128]{2,1,0:T(8,128)(2,1)S(1)}) custom-call(s32[1,19]{1,0:T(1,128)} %prefill_pages_hbm.1, s32[2,4]{1,0:T(2,128)} %decode_pages_hbm.1, s32[2]{0:T(128)} %decode_len_hbm.1, s32[24]{0:T(128)} %overflow_pages_hbm.1, s32[24]{0:T(128)} %overflow_len_hbm.1, ...), custom_call_target="tpu_custom_call" | custom-call | tf_op jit(solution)/shard_map/pallas_call | solution.py:424
  27.0 0.9 %shard_map.131 = (bf16[48,8192]{1,0:T(8,128)(2,1)}, bf16[2,1024]{1,0:T(2,128)(2,1)}, bf16[64,1024]{1,0:T(8,128)(2,1)}) custom-call(bf16[48,8192]{1,0:T(8,128)(2,1)S(1)} %get-tuple-element.6.prefill, bf16[2,1024]{1,0:T(2,128)(2,1)S(1)} %get-tuple-element.7.decode, bf16[64,8,128]{2,1,0:T(8,128)(2,1)S(1)} %get-tuple-element.8.moved), custom_call_target="tpu_custom_call" | custom-call | tf_op jit(solution)/shard_map/pallas_call | solution.py:383
